TPU v7x, 256 devices: a whole 4x4x8 slice. The times are simulated.
256 devices in a mesh: gz: 2 (over core), row: 4 (over x), col: 32 (over z, y).
Axes of the slice: x: 4, y: 4, z: 8, core: 2. Of those that a mesh axis runs over, the one named last changes fastest.
Arguments:
- front_matrix: float32 [4096, 4096], P('row', 'col'), may hold values from -6 to 6
- l_panels: float32 [2, 8, 4, 512, 256], P('gz', None, 'row', 'col'), may hold values from -6 to 6
- l_map: int32 [2, 8, 4, 512], P('gz', None, 'row'), may hold values from 0 to 1024, as said below
- u_panels: float32 [2, 8, 32, 64, 256], P('gz', None, 'col', 'row'), may hold values from -0.375 to 0.375
- u_map: int32 [2, 8, 32, 64], P('gz', None, 'col'), may hold values from 0 to 128, as said below
Outputs:
- updated_front: float32 [4096, 4096], P('row', 'col')
Inputs may be any that keep to these rules, and one draw needn't show every extreme that they name: l_map[z,h,p,:] lists distinct rows of row block p updated by child h of layer z, used slots first, listed block of 128 rows by block, at most 64 rows to a block; unused slots hold 1024; in every child some row block uses all 512 slots. u_map[z,h,q,:] lists distinct columns of column block q updated by child h of layer z, used slots first, listed block of 128 columns by block, at most 64 to a block; unused slots hold 128; in every child some column block uses all 64 slots.
All inputs are finite; a program needn't handle non-finite values.
Results may differ from a plain program's by a relative error of at most 0.0001.
Values sent between devices are 32-bit elements; how exact they have to be, the bound alone decides.
A program may use at most 64 MiB of HBM per device.

v0:
```python
import jax
import jax.numpy as jnp
from jax import lax
from jax.sharding import PartitionSpec as P


def spread_dense(row_panel, row_map, col_dense, row_count):
    targets = jnp.arange(row_count, dtype=jnp.int32)
    narrow = jnp.einsum("hik,hgk->hig", row_panel, col_dense, precision=lax.Precision.HIGHEST)
    row_hot = (row_map[:, :, None] == targets[None, None, :]).astype(jnp.float32)
    return jnp.einsum("hif,hig->fg", row_hot, narrow, precision=lax.Precision.HIGHEST)


def shards(front_matrix, l_panels, l_map, u_panels, u_map):
    row_count, col_count = front_matrix.shape
    row_map = l_map[0, :, 0, :]
    col_map = u_map[0, :, 0, :]
    col_panel = lax.all_gather(u_panels, "row", axis=3, tiled=True)[0, :, 0]
    col_targets = jnp.arange(col_count, dtype=jnp.int32)
    col_hot = (col_map[:, :, None] == col_targets[None, None, :]).astype(jnp.float32)
    col_dense = jnp.einsum("hjg,hjk->hgk", col_hot, col_panel, precision=lax.Precision.HIGHEST)
    row_panel = lax.all_gather(l_panels, "col", axis=3, tiled=True)[0, :, 0]
    update = spread_dense(row_panel, row_map, col_dense, row_count)
    summed = lax.psum(update, "gz")
    return front_matrix - summed


def solution(mesh):
    placed = (
        P("row", "col"),
        P("gz", None, "row", "col", None),
        P("gz", None, "row", None),
        P("gz", None, "col", "row", None),
        P("gz", None, "col", None),
    )
    return jax.shard_map(
        shards, mesh=mesh, in_specs=placed, out_specs=P("row", "col"), check_vma=False
    )
```

profile of v0, /device:TPU:1, one launch (start us, length us, event | category | flops | bytes accessed | tf_op | source)
XLA Modules:
  0.0 145.7 jit_solution(16361774498330991726)
XLA Ops:
  6.5 0.0 all-gather.2.cloned.1.call-start
  6.5 0.7 all-gather.2.cloned.1.call-update
  7.3 0.0 all-reduce.2.cloned.1.call-start
  7.3 0.7 copy.8
  8.0 12.5 %all_gather.6 = f32[1,8,1,64,256]{4,3,2,1,0:T(8,128)S(1)} all-gather(f32[1,8,1,16,256]{4,3,2,1,0:T(8,128)} %param.8), channel_id=1, replica_groups=mesh['gz'=2,'row'=4,'col'=32] {'row'}, dimensions={3}, use_global_device_ids=true | all-gather | bytes 655360 | tf_op jit(solution)/shard_map/all_gather | solution.py:18
  20.6 1.5 %fusion.8 = f32[8,128,256]{2,1,0:T(8,128)S(1)} fusion(f32[1,8,1,64,256]{4,3,2,1,0:T(8,128)S(1)} %all_gather.6, s32[8,64]{1,0:T(8,128)} %bitcast.19), kind=kOutput, calls=%fused_computation.7 | convolution fusion | flops 201392128 | bytes 1574912 | tf_op jit(solution)/shard_map/hjg,hjk->hgk/dot_general | solution.py:21
  22.1 70.8 %all-gather.2.cloned.1.call-done = f32[1,8,1,512,256]{4,3,2,1,0:T(8,128)} async-done(((f32[1,8,1,16,256]{4,3,2,1,0:T(8,128)}), f32[1,8,1,512,256]{4,3,2,1,0:T(8,128)}) %all-gather.2.cloned.1.call-update) | async-done | bytes 4194320 | tf_op jit(solution)/shard_map/all_gather | solution.py:22
  92.9 5.3 %fusion.2 = f32[8,128,512]{1,2,0:T(8,128)S(1)} fusion(f32[8,128,256]{2,1,0:T(8,128)S(1)} %fusion.8, f32[1,8,1,512,256]{4,3,2,1,0:T(8,128)} %all-gather.2.cloned.1.call-done), kind=kOutput, calls=%fused_computation.3 | convolution fusion | flops 1610612736 | bytes 7340032 | tf_op jit(solution)/shard_map/hik,hgk->hig/dot_general | solution.py:9
  98.3 0.0 copy-start
  98.3 8.4 %fusion.5 = f32[1024,128]{1,0:T(8,128)} fusion(f32[8,128,512]{1,2,0:T(8,128)S(1)} %fusion.2, s32[8,512]{1,0:T(8,128)S(1)} %bitcast.18), kind=kOutput, calls=%fused_computation.6 | convolution fusion | flops 6446645248 | bytes 2637824 | tf_op jit(solution)/shard_map/hif,hig->fg/dot_general | solution.py:11
  106.6 0.0 all-reduce.2.cloned.1.call-update
  106.7 30.3 %all-reduce.2.cloned.1.call-done = f32[1024,128]{1,0:T(8,128)} async-done(((f32[1024,128]{1,0:T(8,128)}), f32[1024,128]{1,0:T(8,128)}) %all-reduce.2.cloned.1.call-update) | async-done | bytes 524304 | tf_op jit(solution)/shard_map/psum | solution.py:24
  137.0 0.0 copy-done
  137.0 1.9 %sub.3 = f32[1024,128]{1,0:T(8,128)} subtract(f32[1024,128]{1,0:T(8,128)S(1)} %copy-done, f32[1024,128]{1,0:T(8,128)} %all-reduce.2.cloned.1.call-done) | non-fusion elementwise | flops 131072 | bytes 1572864 | tf_op jit(solution)/shard_map/sub | solution.py:25
Async XLA Ops:
  6.5 86.4 %all-gather.2.cloned.1.call-start = ((), (), s32[]{:S(2)}) async-start(), calls=%async_computation | async-start | bytes 4325376 | tf_op jit(solution)/shard_map/all_gather | solution.py:22
  7.3 129.7 %all-reduce.2.cloned.1.call-start = ((), (), s32[]{:S(2)}) async-start(), calls=%async_computation.1 | async-start | bytes 1048576 | tf_op jit(solution)/shard_map/psum | solution.py:24
  98.3 38.7 %copy-start = (f32[1024,128]{1,0:T(8,128)S(1)}, f32[1024,128]{1,0:T(8,128)}, u32[]{:S(2)}) copy-start(f32[1024,128]{1,0:T(8,128)} %param.5) | copy-start | bytes 1572868
Sparse Core Ops, SparseCore 0:
  9.9 82.9 all-gather.1
  106.8 30.1 all-reduce.1
where the time goes:
time: 146 us
  waiting for transfers between devices  102 us (70%)
  matrix products  15.3 us (10%)
  between operations  13.4 us (9%)
  blocking collectives  12.5 us (9%)
  other arithmetic  1.89 us (1%)
    all_gather x1, waiting for transfers between devices, shards(): row_panel = lax.all_gather(l_panels, 'col', axis=3, tiled=True)[0, :, 0]  70.8 us
    psum x1, waiting for transfers between devices, shards(): summed = lax.psum(update, 'gz')  30.3 us
    all_gather x1, blocking collectives, shards(): col_panel = lax.all_gather(u_panels, 'row', axis=3, tiled=True)[0, :, 0]  12.5 us
    dot_general x1, matrix products, spread_dense(): jnp.einsum('hif,hig->fg', row_hot, narrow, precision=lax.Precision.HIGHEST)  8.37 us
    dot_general x1, matrix products, spread_dense(): jnp.einsum('hik,hgk->hig', row_panel, col_dense, precision=lax.Precision....  5.34 us
  transfers between devices with their start and end apart: 2, of which 2 were waited for; matrix products, arithmetic and copies ran while one was open for 2% of the time, Pallas kernels for 0%

commit v1 on v0

--- a/solution.py
+++ b/solution.py
@@ -1,7 +1,38 @@
+import functools
 import jax
 import jax.numpy as jnp
 from jax import lax
 from jax.sharding import PartitionSpec as P
+
+
+def watch_hubs(local_x, ax_name):
+    n_peers_all = lax.axis_size(ax_name)
+    history = []
+    dev_i = 0
+    while dev_i < n_peers_all:
+        history.append((dev_i, (dev_i + 1) % n_peers_all))
+        dev_i += 1
+    all_rows = []
+    dev_i = 0
+    while dev_i < n_peers_all:
+        all_rows.append((dev_i, (dev_i - 1) % n_peers_all))
+        dev_i += 1
+    local_part, carry_in = ([local_x], [local_x])
+    for _ in range(n_peers_all // 2):
+        current_block = lax.ppermute(local_part[-1], ax_name, history)
+        local_part.append(current_block)
+    j = 0
+    while j < (n_peers_all - 1) // 2:
+        block_out = lax.ppermute(carry_in[-1], ax_name, all_rows)
+        carry_in.append(block_out)
+        j = j + 1
+    y1 = jnp.concatenate([*local_part[::-1], *carry_in[1:]], axis=3)
+    high = lax.axis_index(ax_name)
+    step_out = jnp.roll(y1, (high - n_peers_all // 2) * local_x.shape[3], axis=3)
+    return step_out
+
+
+lift_view = functools.partial(watch_hubs, ax_name="row")
 
 
 def spread_dense(row_panel, row_map, col_dense, row_count):
@@ -15,7 +46,7 @@
     row_count, col_count = front_matrix.shape
     row_map = l_map[0, :, 0, :]
     col_map = u_map[0, :, 0, :]
-    col_panel = lax.all_gather(u_panels, "row", axis=3, tiled=True)[0, :, 0]
+    col_panel = lift_view(u_panels)[0, :, 0]
     col_targets = jnp.arange(col_count, dtype=jnp.int32)
     col_hot = (col_map[:, :, None] == col_targets[None, None, :]).astype(jnp.float32)
     col_dense = jnp.einsum("hjg,hjk->hgk", col_hot, col_panel, precision=lax.Precision.HIGHEST)

time: 146 us -> 146 us (level)
  blocking collectives: 12.5 us -> 0 us
  waiting for transfers between devices: 102 us -> 108 us
  starting transfers between devices: 0.04 us -> 4.83 us
  local copies, waits for them, and re-layouts: 0.73 us -> 2.62 us
    all_gather x1 -> x0, blocking collectives: 12.5 us -> none  [shards(): col_panel = lax.all_gather(u_panels, 'row', axis=3, tiled=True)[0, :, 0]]
    ppermute x0 -> x3, waiting for transfers between devices: none -> 5.47 us  [the longest x2 5.47 us: watch_hubs(): current_block = lax.ppermute(local_part[-1], ax_name, history)]
    ppermute x0 -> x3, starting transfers between devices: none -> 4.79 us  [the longest x1 2.49 us: watch_hubs(): block_out = lax.ppermute(carry_in[-1], ax_name, all_rows)]
    unnamed x3 -> x10, local copies, waits for them, and re-layouts: 0.73 us -> 2.61 us
  transfers between devices with their start and end apart: 2 -> 5, of which waited for: 2 -> 4; matrix products, arithmetic and copies ran while one was open for 2% -> 3% of each run, Pallas kernels for 0% -> 0%
where the time goes in v1:
time: 146 us
  waiting for transfers between devices  108 us (74%)
  matrix products  15.3 us (10%)
  between operations  13.5 us (9%)
  starting transfers between devices  4.83 us (3%)
  local copies, waits for them, and re-layouts  2.62 us (2%)
  other arithmetic  1.89 us (1%)
    all_gather x1, waiting for transfers between devices, shards(): row_panel = lax.all_gather(l_panels, 'col', axis=3, tiled=True)[0, :, 0]  71.1 us
    psum x1, waiting for transfers between devices, shards(): summed = lax.psum(update, 'gz')  30.3 us
    dot_general x1, matrix products, spread_dense(): jnp.einsum('hif,hig->fg', row_hot, narrow, precision=lax.Precision.HIGHEST)  8.37 us
    ppermute x2, waiting for transfers between devices, watch_hubs(): current_block = lax.ppermute(local_part[-1], ax_name, history)  5.47 us
    dot_general x1, matrix products, spread_dense(): jnp.einsum('hik,hgk->hig', row_panel, col_dense, precision=lax.Precision....  5.34 us
  transfers between devices with their start and end apart: 5, of which 4 were waited for; matrix products, arithmetic and copies ran while one was open for 3% of the time, Pallas kernels for 0%

profile of v1, /device:TPU:1, one launch (start us, length us, event | category | flops | bytes accessed | tf_op | source)
XLA Modules:
  0.0 145.7 jit_solution(486036263171237921)
XLA Ops:
  6.5 0.0 all-gather.2.cloned.1.call-start
  6.5 0.7 all-gather.2.cloned.1.call-update
  7.3 0.0 all-reduce.2.cloned.1.call-start
  7.3 2.1 %collective-permute-start = (f32[1,8,1,16,256]{4,3,2,1,0:T(8,128)}, f32[1,8,1,16,256]{4,3,2,1,0:T(8,128)S(1)}, u32[]{:S(2)}, u32[]{:S(2)}) collective-permute-start(f32[1,8,1,16,256]{4,3,2,1,0:T(8,128)} %param.8), channel_id=1, source_target_pairs={{0,32},{32,64},{64,96},{96,0},{1,33},{33,65},{65,97},{97,1},{2,34}... | collective-permute-start | bytes 393224 | tf_op jit(solution)/shard_map/ppermute | solution.py:22
  9.4 3.8 %collective-permute-done = f32[1,8,1,16,256]{4,3,2,1,0:T(8,128)S(1)} collective-permute-done((f32[1,8,1,16,256]{4,3,2,1,0:T(8,128)}, f32[1,8,1,16,256]{4,3,2,1,0:T(8,128)S(1)}, u32[]{:S(2)}, u32[]{:S(2)}) %collective-permute-start) | collective-permute-done | bytes 131104 | tf_op jit(solution)/shard_map/ppermute | solution.py:22
  13.3 0.2 collective-permute-start.1
  13.4 2.5 %collective-permute-start.2 = (f32[1,8,1,16,256]{4,3,2,1,0:T(8,128)}, f32[1,8,1,16,256]{4,3,2,1,0:T(8,128)S(1)}, u32[]{:S(2)}, u32[]{:S(2)}) collective-permute-start(f32[1,8,1,16,256]{4,3,2,1,0:T(8,128)} %param.8), channel_id=1, source_target_pairs={{0,96},{32,0},{64,32},{96,64},{1,97},{33,1},{65,33},{97,65},{2,98}... | collective-permute-start | bytes 393224 | tf_op jit(solution)/shard_map/ppermute | solution.py:26
  15.9 0.7 copy.8
  16.7 1.6 %collective-permute-done.1 = f32[1,8,1,16,256]{4,3,2,1,0:T(8,128)S(1)} collective-permute-done((f32[1,8,1,16,256]{4,3,2,1,0:T(8,128)S(1)}, f32[1,8,1,16,256]{4,3,2,1,0:T(8,128)S(1)}, u32[]{:S(2)}, u32[]{:S(2)}) %collective-permute-start.1) | collective-permute-done | bytes 131104 | tf_op jit(solution)/shard_map/ppermute | solution.py:22
  18.3 0.9 constant_dynamic-update-slice_fusion.5
  19.2 0.0 collective-permute-done.2
  19.3 0.9 constant_dynamic-update-slice_fusion.1
  20.2 1.6 %fusion.8 = f32[8,128,256]{2,1,0:T(8,128)S(1)} fusion(f32[1,8,1,128,256]{4,3,2,1,0:T(8,128)S(1)} %constant_dynamic-update-slice_fusion, s32[]{:T(128)S(6)} %select_n.14, s32[8,64]{1,0:T(8,128)} %bitcast.19), kind=kOutput, calls=%fused_computation.7 | convolution fusion | flops 201392128 | bytes 1574916 | tf_op jit(solution)/shard_map/hjg,hjk->hgk/dot_general | solution.py:52
  21.8 71.1 %all-gather.2.cloned.1.call-done = f32[1,8,1,512,256]{4,3,2,1,0:T(8,128)} async-done(((f32[1,8,1,16,256]{4,3,2,1,0:T(8,128)}), f32[1,8,1,512,256]{4,3,2,1,0:T(8,128)}) %all-gather.2.cloned.1.call-update) | async-done | bytes 4194320 | tf_op jit(solution)/shard_map/all_gather | solution.py:53
  92.9 5.3 %fusion.2 = f32[8,128,512]{1,2,0:T(8,128)S(1)} fusion(f32[8,128,256]{2,1,0:T(8,128)S(1)} %fusion.8, f32[1,8,1,512,256]{4,3,2,1,0:T(8,128)} %all-gather.2.cloned.1.call-done), kind=kOutput, calls=%fused_computation.3 | convolution fusion | flops 1610612736 | bytes 7340032 | tf_op jit(solution)/shard_map/hik,hgk->hig/dot_general | solution.py:40
  98.3 0.0 copy-start
  98.3 8.4 %fusion.5 = f32[1024,128]{1,0:T(8,128)} fusion(f32[8,128,512]{1,2,0:T(8,128)S(1)} %fusion.2, s32[8,512]{1,0:T(8,128)S(1)} %bitcast.18), kind=kOutput, calls=%fused_computation.6 | convolution fusion | flops 6446645248 | bytes 2637824 | tf_op jit(solution)/shard_map/hif,hig->fg/dot_general | solution.py:42
  106.6 0.0 all-reduce.2.cloned.1.call-update
  106.7 30.3 %all-reduce.2.cloned.1.call-done = f32[1024,128]{1,0:T(8,128)} async-done(((f32[1024,128]{1,0:T(8,128)}), f32[1024,128]{1,0:T(8,128)}) %all-reduce.2.cloned.1.call-update) | async-done | bytes 524304 | tf_op jit(solution)/shard_map/psum | solution.py:55
  137.0 0.0 copy-done
  137.0 1.9 %sub.12 = f32[1024,128]{1,0:T(8,128)} subtract(f32[1024,128]{1,0:T(8,128)S(1)} %copy-done, f32[1024,128]{1,0:T(8,128)} %all-reduce.2.cloned.1.call-done) | non-fusion elementwise | flops 131072 | bytes 1572864 | tf_op jit(solution)/shard_map/sub | solution.py:56
  (6 shorter events, 0.1 us)
Async XLA Ops:
  6.5 86.4 %all-gather.2.cloned.1.call-start = ((), (), s32[]{:S(2)}) async-start(), calls=%async_computation | async-start | bytes 4325376 | tf_op jit(solution)/shard_map/all_gather | solution.py:53
  7.3 129.7 %all-reduce.2.cloned.1.call-start = ((), (), s32[]{:S(2)}) async-start(), calls=%async_computation.1 | async-start | bytes 1048576 | tf_op jit(solution)/shard_map/psum | solution.py:55
  7.3 6.0 %collective-permute-start = (f32[1,8,1,16,256]{4,3,2,1,0:T(8,128)}, f32[1,8,1,16,256]{4,3,2,1,0:T(8,128)S(1)}, u32[]{:S(2)}, u32[]{:S(2)}) collective-permute-start(f32[1,8,1,16,256]{4,3,2,1,0:T(8,128)} %param.8), channel_id=1, source_target_pairs={{0,32},{32,64},{64,96},{96,0},{1,33},{33,65},{65,97},{97,1},{2,34}... | collective-permute-start | bytes 393224 | tf_op jit(solution)/shard_map/ppermute | solution.py:22
  13.3 5.0 %collective-permute-start.1 = (f32[1,8,1,16,256]{4,3,2,1,0:T(8,128)S(1)}, f32[1,8,1,16,256]{4,3,2,1,0:T(8,128)S(1)}, u32[]{:S(2)}, u32[]{:S(2)}) collective-permute-start(f32[1,8,1,16,256]{4,3,2,1,0:T(8,128)S(1)} %collective-permute-done), channel_id=1, source_target_pairs={{0,32},{32,64},{64,96},{96,0},{1,33},{33,65},{65,97},{97,1},{2,34}... | collective-permute-start | bytes 393224 | tf_op jit(solution)/shard_map/ppermute | solution.py:22
  13.4 5.8 %collective-permute-start.2 = (f32[1,8,1,16,256]{4,3,2,1,0:T(8,128)}, f32[1,8,1,16,256]{4,3,2,1,0:T(8,128)S(1)}, u32[]{:S(2)}, u32[]{:S(2)}) collective-permute-start(f32[1,8,1,16,256]{4,3,2,1,0:T(8,128)} %param.8), channel_id=1, source_target_pairs={{0,96},{32,0},{64,32},{96,64},{1,97},{33,1},{65,33},{97,65},{2,98}... | collective-permute-start | bytes 393224 | tf_op jit(solution)/shard_map/ppermute | solution.py:26
  98.3 38.7 %copy-start = (f32[1024,128]{1,0:T(8,128)S(1)}, f32[1024,128]{1,0:T(8,128)}, u32[]{:S(2)}) copy-start(f32[1024,128]{1,0:T(8,128)} %param.5) | copy-start | bytes 1572868
Sparse Core Ops, SparseCore 0:
  9.9 82.9 all-gather.1
  106.8 30.1 all-reduce.1
